TPU v7x, 256 devices: a whole 4x4x8 slice. The times are simulated.
256 devices in a mesh: section: 4 (over y), ctx: 64 (over z, x, core).
Axes of the slice: x: 4, y: 4, z: 8, core: 2. Of those that a mesh axis runs over, the one named last changes fastest.
Arguments:
- incoming: bfloat16 [4, 8192, 4096], P('section', 'ctx'), may hold values from -6 to 6
- layer_input: bfloat16 [4, 8192, 4096], P('section', 'ctx'), may hold values from -6 to 6
- pre_gate: bfloat16 [4, 8192, 4096], P('section', 'ctx'), may hold values from -6 to 6
- mid_gate: bfloat16 [4, 8192, 4096], P('section', 'ctx'), may hold values from -6 to 6
- long_gate: bfloat16 [4, 8192, 4096], P('section', 'ctx'), may hold values from -6 to 6
- out_gate: bfloat16 [4, 8192, 4096], P('section', 'ctx'), may hold values from -6 to 6
- long_filter: bfloat16 [4, 4096, 8192], P('section', 'ctx'), may hold values from -0.0625 to 0.0625
- mid_filter: bfloat16 [4, 128, 4096], P('section'), may hold values from -0.5 to 0.5
Outputs:
- input_grad: bfloat16 [4, 8192, 4096], P('section', 'ctx')
- long_grad: bfloat16 [4, 4096, 8192], P('section', 'ctx')
- mid_grad: bfloat16 [4, 128, 4096], P('section', None, 'ctx')
All inputs are finite; a program needn't handle non-finite values.
Results may differ from a plain program's by a relative error of at most 0.008.
Values may be sent and summed in bfloat16 or wider, within the bound.
A program may use at most 192 MiB of HBM per device.

v0:
```python
import math
import jax
import jax.numpy as jnp
from jax import lax
from jax.sharding import PartitionSpec as P


def passed_along(value, axis, steps):
    count = lax.axis_size(axis)
    pairs = [(source, (source + steps) % count) for source in range(count)]
    return lax.ppermute(value, axis, pairs)


def shifted(array, axis, by):
    devices = lax.axis_size(axis)
    pairs = [(i, i + by) for i in range(devices) if 0 <= i + by < devices]
    return lax.ppermute(array, axis, pairs)


def unit_roots(rows, cols, period):
    row_ids = jnp.arange(rows, dtype=jnp.int32)[:, None]
    col_ids = jnp.arange(cols, dtype=jnp.int32)[None, :]
    angle = (row_ids * col_ids % period).astype(jnp.float32) * (-2.0 * math.pi / period)
    return (jnp.cos(angle), jnp.sin(angle))


def contract(form, left, right):
    return jnp.einsum(
        form, left, right, precision=lax.Precision.HIGH, preferred_element_type=jnp.float32
    )


def to_spectrum(parts, factor_a, factor_b):
    channels = parts.shape[0]
    inputs_count = parts.shape[1]
    half = factor_a // 2
    period = factor_a * factor_b
    fa_cos, fa_sin = unit_roots(factor_a, half, factor_a)
    first_table = jnp.stack([jnp.stack([fa_cos, -fa_sin]), jnp.stack([fa_sin, fa_cos])])[
        :, :inputs_count
    ]
    tw_cos, tw_sin = unit_roots(factor_a, factor_b, period)
    fb_cos, fb_sin = unit_roots(factor_b, factor_b, factor_b)
    second_table = jnp.stack([jnp.stack([fb_cos, fb_sin]), jnp.stack([-fb_sin, fb_cos])])
    shaped = parts.reshape(channels, inputs_count, half, factor_b)
    first = contract("qrca,nrab->nqcb", first_table, shaped)
    first_re = first[:, 0]
    first_im = first[:, 1]
    turned = jnp.stack(
        [first_re * tw_cos - first_im * tw_sin, first_re * tw_sin + first_im * tw_cos], 1
    )
    return contract("nqcb,qpbd->npcd", turned, second_table)


def from_spectrum(spectrum, factor_a, factor_b, scale):
    channels = spectrum.shape[0]
    half = factor_a // 2
    period = factor_a * factor_b
    fb_cos, fb_sin = unit_roots(factor_b, factor_b, factor_b)
    back_table = jnp.stack([jnp.stack([fb_cos, -fb_sin]), jnp.stack([fb_sin, fb_cos])])
    tw_cos, tw_sin = unit_roots(factor_a, factor_b, period)
    fa_cos, fa_sin = unit_roots(half, factor_a, factor_a)
    last_table = jnp.stack(
        [
            jnp.stack([fa_cos, fa_sin]) * (scale / period),
            jnp.stack([-fa_sin, fa_cos]) * (1.0 / period),
        ]
    )
    middle = contract("npcd,pqdb->nqcb", spectrum, back_table)
    middle_re = middle[:, 0]
    middle_im = middle[:, 1]
    turned = jnp.stack(
        [middle_re * tw_cos + middle_im * tw_sin, middle_im * tw_cos - middle_re * tw_sin], 1
    )
    result = contract("rqac,nqcb->nrab", last_table, turned)
    length = half * factor_b
    return (result[:, 0].reshape(channels, length), result[:, 1].reshape(channels, length))


def depthwise(extended, kernel):
    result = lax.conv_general_dilated(
        extended[None],
        kernel[:, None, :],
        (1,),
        "VALID",
        dimension_numbers=("NWC", "WIO", "NWC"),
        feature_group_count=extended.shape[1],
        preferred_element_type=jnp.float32,
    )
    return result[0]


def per_device(
    incoming, layer_input, pre_gate, mid_gate, long_gate, out_gate, long_filter, mid_filter
):
    sections = lax.axis_size("section")
    beta = (2.0 * sections) ** (-0.5)
    adjoint = passed_along(incoming[0], "section", -1).astype(jnp.float32)
    inputs = layer_input[0].astype(jnp.float32)
    tokens = inputs.shape[0]
    gate_pre = pre_gate[0].astype(jnp.float32)
    gate_mid = mid_gate[0].astype(jnp.float32)
    gate_long = long_gate[0].astype(jnp.float32)
    gate_out = out_gate[0].astype(jnp.float32)
    filter_taps = mid_filter[0]
    reach = filter_taps.shape[0] - 1
    seq_len = tokens * lax.axis_size("ctx")
    scale = float(seq_len) ** (-0.5)
    mixed_in = (inputs * gate_pre).astype(jnp.bfloat16)
    earlier = shifted(mixed_in[tokens - reach :], "ctx", 1)
    extended = jnp.concatenate([earlier, mixed_in], 0)
    branch = depthwise(extended, filter_taps[::-1])
    resid = inputs + beta * branch * gate_mid
    long_in = (resid * gate_long).astype(jnp.bfloat16)
    grad_z = (beta * adjoint * gate_out).astype(jnp.bfloat16)
    channel_z, channel_w = (
        lax.all_to_all(grad_z.T, "ctx", split_axis=0, concat_axis=1, tiled=True),
        lax.all_to_all(long_in.T, "ctx", split_axis=0, concat_axis=1, tiled=True),
    )
    factor_b = math.gcd(seq_len, 128)
    factor_a = 2 * seq_len // factor_b
    zspec = to_spectrum(channel_z[:, None], factor_a, factor_b)
    zspec_re = zspec[:, 0]
    zspec_im = zspec[:, 1]
    pair = to_spectrum(jnp.stack([channel_w, -long_filter[0]], 1), factor_a, factor_b)
    pair_re = pair[:, 0]
    pair_im = pair[:, 1]
    joint_re = zspec_re * pair_re + zspec_im * pair_im
    joint_im = zspec_im * pair_re - zspec_re * pair_im
    lag_grad, input_part = from_spectrum(
        jnp.stack([joint_re, joint_im], 1), factor_a, factor_b, scale
    )
    long_grad = lag_grad.astype(jnp.bfloat16)[None]
    returned = lax.all_to_all(
        input_part.astype(jnp.bfloat16), "ctx", split_axis=1, concat_axis=0, tiled=True
    ).T
    grad_u = adjoint + returned.astype(jnp.float32) * gate_long
    grad_b = (beta * grad_u * gate_mid).astype(jnp.bfloat16)
    later = shifted(grad_b[:reach], "ctx", -1)
    grad_act = depthwise(jnp.concatenate([grad_b, later], 0), filter_taps)
    input_grad = (grad_u + grad_act * gate_pre).astype(jnp.bfloat16)[None]
    tap_part = depthwise(extended, grad_b)[::-1]
    total_taps = lax.psum(tap_part, "ctx")
    columns = tap_part.shape[1] // lax.axis_size("ctx")
    own_taps = lax.dynamic_slice_in_dim(total_taps, lax.axis_index("ctx") * columns, columns, 1)
    mid_grad = (own_taps * scale).astype(jnp.bfloat16)[None]
    return (input_grad, long_grad, mid_grad)


def solution(mesh):
    placed = (
        P("section", "ctx", None),
        P("section", "ctx", None),
        P("section", "ctx", None),
        P("section", "ctx", None),
        P("section", "ctx", None),
        P("section", "ctx", None),
        P("section", "ctx", None),
        P("section", None, None),
    )
    return jax.shard_map(
        per_device,
        mesh=mesh,
        in_specs=placed,
        out_specs=(P("section", "ctx", None), P("section", "ctx", None), P("section", None, "ctx")),
        check_vma=False,
    )
```

profile of v0, /device:TPU:8, one launch (start us, length us, event | category | flops | bytes accessed | tf_op | source)
XLA Modules:
  0.0 467.0 jit_solution(479754405011131320)
XLA Ops:
  7.2 1.9 fusion.24
  9.1 1.2 slice.67
  10.3 2.7 collective-permute-start.1
  13.0 1.2 rev.6
  14.2 0.4 collective-permute-done.1
  14.6 1.6 maximum_bitcast_fusion.13
  16.3 27.4 %convolution_multiply_fusion = f32[1,128,4096]{2,0,1:T(1,128)S(1)} fusion(bf16[1,255,4096]{2,1,0:T(8,128)(2,1)S(1)} %maximum_bitcast_fusion.13, bf16[128,1,4096]{2,0,1:T(8,128)(2,1)S(1)} %bitcast.188), kind=kOutput, calls=%fused_computation.15 | convolution fusion | flops 134742016 | bytes 5234688 | tf_op jit(solution)/shard_map/conv_general_dilated | solution.py:81
  43.7 2.1 fusion.34
  45.8 1.3 copy.57
  47.1 24.9 %all-to-all-start.1 = ((bf16[64,64,128]{2,1,0:T(8,128)(2,1)}), bf16[64,64,128]{2,1,0:T(8,128)(2,1)S(1)}, u32[]{:S(2)}, u32[]{:S(2)}) async-start(bf16[64,64,128]{2,1,0:T(8,128)(2,1)} %bitcast.35), calls=%async_computation.1 | async-start | bytes 2097152 | tf_op jit(solution)/shard_map/all_to_all | solution.py:118
  72.0 0.5 collective-permute-start
  72.5 24.9 %collective-permute-done = bf16[128,4096]{1,0:T(8,128)(2,1)S(1)} collective-permute-done((bf16[128,4096]{1,0:T(8,128)(2,1)}, bf16[128,4096]{1,0:T(8,128)(2,1)S(1)}, u32[]{:S(2)}, u32[]{:S(2)}) %collective-permute-start) | collective-permute-done | bytes 1048608 | tf_op jit(solution)/shard_map/ppermute | solution.py:11
  97.4 1.9 fusion.36
  99.3 1.3 copy.51
  100.9 10.9 %all-to-all-start = ((bf16[64,64,128]{2,1,0:T(8,128)(2,1)}), bf16[64,64,128]{2,1,0:T(8,128)(2,1)}, u32[]{:S(2)}, u32[]{:S(2)}) async-start(bf16[64,64,128]{2,1,0:T(8,128)(2,1)} %bitcast.183), calls=%async_computation | async-start | bytes 2097152 | tf_op jit(solution)/shard_map/all_to_all | solution.py:117
  111.8 1.4 negate_bitcast_fusion
  114.3 0.3 fusion.73
  114.6 0.3 fusion.77
  114.9 0.7 maximum_multiply_fusion
  115.6 0.7 fusion.43
  116.3 0.7 copy.132
  117.0 5.7 %convolution_bitcast_fusion.1 = f32[64,2,128,128]{2,3,1,0:T(8,128)} fusion(bf16[64,1,64,128]{3,2,1,0:T(8,128)(2,1)S(1)} %bitcast.184, bf16[64,1,64,128]{3,2,1,0:T(8,128)(2,1)S(1)} %bitcast.185, f32[1,2,128,64]{2,3,0,1:T(8,128)S(1)} %get-tuple-element.33, f32[1,2,128,64]{2,3,0,1:T(8,128)S(1)} %get-tuple-element.32), kind=kOutput, calls=%fused_computation.34 | convolution fusion | flops 1614839808 | bytes 10616832 | tf_op jit(solution)/shard_map/qrca,nrab->nqcb/dot_general | solution.py:28
  122.7 17.8 %all-to-all-done = bf16[64,64,128]{2,1,0:T(8,128)(2,1)} async-done(((bf16[64,64,128]{2,1,0:T(8,128)(2,1)}), bf16[64,64,128]{2,1,0:T(8,128)(2,1)}, u32[]{:S(2)}, u32[]{:S(2)}) %all-to-all-start) | async-done | bytes 1048608 | tf_op jit(solution)/shard_map/all_to_all | solution.py:117
  140.5 3.8 convolution_bitcast_fusion
  144.3 5.8 %multiply_subtract_fusion.3 = (f32[64,1,128,128]{2,3,1,0:T(8,128)}, f32[64,1,128,128]{2,3,1,0:T(8,128)}, f32[64,1,128,128]{2,3,1,0:T(8,128)S(1)}, f32[64,1,128,128]{2,3,1,0:T(8,128)}) fusion(f32[64,2,128,128]{2,3,1,0:T(8,128)S(1)} %convolution_bitcast_fusion, f32[128,128]{0,1:T(8,128)S(1)} %get-tuple-element.36, f32[128,128]{0,1:T(8,128)S(1)} %get-tuple-element.37, ...), kind=kLoop, calls=%fused_computation.24 | loop fusion | flops 12582912 | bytes 33685504 | tf_op jit(solution)/shard_map/sub | solution.py:50
  150.1 7.0 %fusion.20 = f32[64,2,128,128]{2,3,0,1:T(8,128)S(1)} fusion(f32[64,1,128,128]{2,3,1,0:T(8,128)} %get-tuple-element.17, f32[64,1,128,128]{2,3,1,0:T(8,128)} %get-tuple-element.16, f32[1,2,128,128]{2,3,0,1:T(8,128)S(1)} %get-tuple-element.23, f32[1,2,128,128]{2,3,0,1:T(8,128)S(1)} %get-tuple-element.28), kind=kOutput, calls=%fused_computation.33 | convolution fusion | flops 3223388160 | bytes 17039360 | tf_op jit(solution)/shard_map/nqcb,qpbd->npcd/dot_general | solution.py:28
  157.1 4.9 %fusion.19 = f32[64,2,128,128]{2,3,0,1:T(8,128)S(1)} fusion(f32[64,1,128,128]{2,3,1,0:T(8,128)S(1)} %get-tuple-element.26, f32[64,1,128,128]{2,3,1,0:T(8,128)S(1)} %copy-done.3, f32[1,2,128,128]{2,3,0,1:T(8,128)S(1)} %get-tuple-element.23, f32[1,2,128,128]{2,3,0,1:T(8,128)S(1)} %get-tuple-element.28), kind=kOutput, calls=%fused_computation.32 | convolution fusion | flops 3223388160 | bytes 17039360 | tf_op jit(solution)/shard_map/nqcb,qpbd->npcd/dot_general | solution.py:28
  162.1 1.8 multiply_add_fusion.1
  163.9 5.0 %fusion.16 = f32[64,2,128,128]{2,3,1,0:T(8,128)S(1)} fusion(f32[64,1,128,128]{2,3,0,1:T(8,128)S(1)} %get-tuple-element.13, f32[64,1,128,128]{2,3,0,1:T(8,128)S(1)} %get-tuple-element.12, f32[1,2,128,128]{2,3,1,0:T(8,128)S(1)} %copy-done.20, f32[1,2,128,128]{2,3,1,0:T(8,128)S(1)} %copy-done.19), kind=kOutput, calls=%fused_computation.30 | convolution fusion | flops 3223388160 | bytes 17039360 | tf_op jit(solution)/shard_map/npcd,pqdb->nqcb/dot_general | solution.py:28
  168.9 1.9 multiply_add_fusion
  170.9 4.6 fusion.33
  175.7 1.6 copy.65
  177.3 5.6 %all-to-all-start.2 = ((bf16[64,64,128]{2,0,1:T(8,128)(2,1)}), bf16[64,64,128]{2,0,1:T(8,128)(2,1)S(1)}, u32[]{:S(2)}, u32[]{:S(2)}) async-start(bf16[64,64,128]{2,0,1:T(8,128)(2,1)} %copy.65), calls=%async_computation.2 | async-start | bytes 2097152 | tf_op jit(solution)/shard_map/all_to_all | solution.py:134
  183.0 1.3 convert_element_type.242
  184.2 27.6 %all-to-all-done.2 = bf16[64,64,128]{2,0,1:T(8,128)(2,1)S(1)} async-done(((bf16[64,64,128]{2,0,1:T(8,128)(2,1)}), bf16[64,64,128]{2,0,1:T(8,128)(2,1)S(1)}, u32[]{:S(2)}, u32[]{:S(2)}) %all-to-all-start.2) | async-done | bytes 1048608 | tf_op jit(solution)/shard_map/all_to_all | solution.py:134
  211.8 1.6 convert_element_type.251
  213.4 1.9 copy.66
  215.4 3.9 fusion.23
  219.2 1.3 collective-permute-start.2
  220.5 28.8 %fusion.13 = f32[1,128,4096]{2,0,1:T(1,128)S(1)} fusion(bf16[1,255,4096]{2,1,0:T(8,128)(2,1)S(1)} %copy-done.12, bf16[128,1,4096]{2,0,1:T(8,128)(2,1)} %bitcast.72), kind=kOutput, calls=%fused_computation.27 | convolution fusion | flops 134217728 | bytes 5234688 | tf_op jit(solution)/shard_map/conv_general_dilated | solution.py:81
  249.3 3.0 copy.131
  252.3 16.6 %rev.7 = f32[128,4096]{1,0:T(8,128)} reverse(f32[128,4096]{1,0:T(8,128)} %bitcast.182), dimensions={0} | reverse | bytes 4194304 | tf_op jit(solution)/shard_map/rev | solution.py:142
  269.0 1.5 maximum_bitcast_fusion.16
  270.6 30.1 %fusion.11 = f32[1,128,4096]{2,0,1:T(1,128)S(1)} fusion(bf16[1,255,4096]{2,1,0:T(8,128)(2,1)S(1)} %maximum_bitcast_fusion.16, bf16[128,1,4096]{2,0,1:T(8,128)(2,1)S(1)} %bitcast.187), kind=kOutput, calls=%fused_computation.25 | convolution fusion | flops 134217728 | bytes 5234688 | tf_op jit(solution)/shard_map/conv_general_dilated | solution.py:81
  300.7 2.8 fusion.35
  303.6 154.7 %all-reduce.2.cloned.1.call-done = f32[128,4096]{1,0:T(8,128)} async-done(((f32[128,4096]{1,0:T(8,128)}), f32[128,4096]{1,0:T(8,128)}) %all-reduce.2.cloned.1.call-update) | async-done | bytes 2097168 | tf_op jit(solution)/shard_map/psum | solution.py:143
  458.3 0.9 fusion.70
  459.2 0.7 copy.71
  (54 shorter events, 1.7 us)
Async XLA Ops:
  7.2 5.9 %copy-start.13 = (bf16[1,128,4096]{2,1,0:T(8,128)(2,1)S(1)}, bf16[1,128,4096]{2,1,0:T(8,128)(2,1)}, u32[]{:S(2)}) copy-start(bf16[1,128,4096]{2,1,0:T(8,128)(2,1)} %param.15) | copy-start | bytes 3145732
  10.3 4.3 collective-permute-start.1
  16.2 27.5 %copy-start.11 = (bf16[1,255,4096]{2,1,0:T(8,128)(2,1)}, bf16[1,255,4096]{2,1,0:T(8,128)(2,1)S(1)}, u32[]{:S(2)}) copy-start(bf16[1,255,4096]{2,1,0:T(8,128)(2,1)S(1)} %maximum_bitcast_fusion.13) | copy-start | bytes 6266884
  16.2 27.5 %copy-start.6 = (bf16[1,128,4096]{2,1,0:T(8,128)(2,1)S(1)}, bf16[1,128,4096]{2,1,0:T(8,128)(2,1)}, u32[]{:S(2)}) copy-start(bf16[1,128,4096]{2,1,0:T(8,128)(2,1)} %param.12) | copy-start | bytes 3145732
  16.2 27.5 %copy-start.8 = (bf16[1,128,4096]{2,1,0:T(8,128)(2,1)S(1)}, bf16[1,128,4096]{2,1,0:T(8,128)(2,1)}, u32[]{:S(2)}) copy-start(bf16[1,128,4096]{2,1,0:T(8,128)(2,1)} %param.9) | copy-start | bytes 3145732
  16.2 27.5 %copy-start.9 = (bf16[1,128,4096]{2,1,0:T(8,128)(2,1)S(1)}, bf16[1,128,4096]{2,1,0:T(8,128)(2,1)}, u32[]{:S(2)}) copy-start(bf16[1,128,4096]{2,1,0:T(8,128)(2,1)} %param.11) | copy-start | bytes 3145732
  47.1 53.8 %all-to-all-start.1 = ((bf16[64,64,128]{2,1,0:T(8,128)(2,1)}), bf16[64,64,128]{2,1,0:T(8,128)(2,1)S(1)}, u32[]{:S(2)}, u32[]{:S(2)}) async-start(bf16[64,64,128]{2,1,0:T(8,128)(2,1)} %bitcast.35), calls=%async_computation.1 | async-start | bytes 2097152 | tf_op jit(solution)/shard_map/all_to_all | solution.py:118
  72.0 25.4 %collective-permute-start = (bf16[128,4096]{1,0:T(8,128)(2,1)}, bf16[128,4096]{1,0:T(8,128)(2,1)S(1)}, u32[]{:S(2)}, u32[]{:S(2)}) collective-permute-start(bf16[128,4096]{1,0:T(8,128)(2,1)} %bitcast.189), channel_id=1, source_target_pairs={{0,192},{64,0},{128,64},{192,128},{1,193},{65,1},{129,65},{193,129... | collective-permute-start | bytes 3145736 | tf_op jit(solution)/shard_map/ppermute | solution.py:11
  97.4 117.9 %copy-start.4 = (bf16[128,4096]{1,0:T(8,128)(2,1)}, bf16[128,4096]{1,0:T(8,128)(2,1)S(1)}, u32[]{:S(2)}) copy-start(bf16[128,4096]{1,0:T(8,128)(2,1)S(1)} %collective-permute-done) | copy-start | bytes 3145732
  100.9 39.6 %all-to-all-start = ((bf16[64,64,128]{2,1,0:T(8,128)(2,1)}), bf16[64,64,128]{2,1,0:T(8,128)(2,1)}, u32[]{:S(2)}, u32[]{:S(2)}) async-start(bf16[64,64,128]{2,1,0:T(8,128)(2,1)} %bitcast.183), calls=%async_computation | async-start | bytes 2097152 | tf_op jit(solution)/shard_map/all_to_all | solution.py:117
  114.9 2.1 copy-start.15
  114.9 2.1 copy-start.16
  140.5 3.8 copy-start
  150.1 7.0 %copy-start.3 = (f32[64,1,128,128]{2,3,1,0:T(8,128)S(1)}, f32[64,1,128,128]{2,3,1,0:T(8,128)}, u32[]{:S(2)}) copy-start(f32[64,1,128,128]{2,3,1,0:T(8,128)} %get-tuple-element.27) | copy-start | bytes 12582916
  162.0 1.9 copy-start.19
  162.1 1.9 copy-start.20
  168.9 1.9 copy-start.17
  168.9 1.9 copy-start.18
  177.3 34.5 %all-to-all-start.2 = ((bf16[64,64,128]{2,0,1:T(8,128)(2,1)}), bf16[64,64,128]{2,0,1:T(8,128)(2,1)S(1)}, u32[]{:S(2)}, u32[]{:S(2)}) async-start(bf16[64,64,128]{2,0,1:T(8,128)(2,1)} %copy.65), calls=%async_computation.2 | async-start | bytes 2097152 | tf_op jit(solution)/shard_map/all_to_all | solution.py:134
  182.9 275.3 %all-reduce.2.cloned.1.call-start = ((), (), s32[]{:S(2)}) async-start(), calls=%async_computation.3 | async-start | bytes 4194304 | tf_op jit(solution)/shard_map/psum | solution.py:143
  215.3 34.0 %copy-start.1 = (f32[4096,128]{0,1:T(8,128)}, f32[4096,128]{0,1:T(8,128)S(1)}, u32[]{:S(2)}) copy-start(f32[4096,128]{0,1:T(8,128)S(1)} %copy.66) | copy-start | bytes 6291460
  215.3 5.2 %copy-start.12 = (bf16[1,255,4096]{2,1,0:T(8,128)(2,1)S(1)}, bf16[1,255,4096]{2,1,0:T(8,128)(2,1)}, u32[]{:S(2)}) copy-start(bf16[1,255,4096]{2,1,0:T(8,128)(2,1)} %copy-done.11) | copy-start | bytes 6266884
  219.2 49.7 %collective-permute-start.2 = (bf16[127,4096]{1,0:T(8,128)(2,1)}, bf16[127,4096]{1,0:T(8,128)(2,1)S(1)}, u32[]{:S(2)}, u32[]{:S(2)}) collective-permute-start(bf16[127,4096]{1,0:T(8,128)(2,1)} %bitcast.180), channel_id=1, source_target_pairs={{1,0},{2,1},{3,2},{4,3},{5,4},{6,5},{7,6},{8,7},{9,8},{10,9},{11,1... | collective-permute-start | bytes 3121160 | tf_op jit(solution)/shard_map/ppermute | solution.py:17
  268.9 1.6 copy-start.14
  270.5 30.2 %copy-start.2 = (f32[4096,128]{0,1:T(8,128)S(1)}, f32[4096,128]{0,1:T(8,128)}, u32[]{:S(2)}) copy-start(f32[4096,128]{0,1:T(8,128)} %copy-done.1) | copy-start | bytes 6291460
  270.5 30.2 %copy-start.5 = (bf16[128,4096]{1,0:T(8,128)(2,1)S(1)}, bf16[128,4096]{1,0:T(8,128)(2,1)}, u32[]{:S(2)}) copy-start(bf16[128,4096]{1,0:T(8,128)(2,1)} %copy-done.4) | copy-start | bytes 3145732
  270.6 30.2 %copy-start.7 = (bf16[1,128,4096]{2,1,0:T(8,128)(2,1)S(1)}, bf16[1,128,4096]{2,1,0:T(8,128)(2,1)}, u32[]{:S(2)}) copy-start(bf16[1,128,4096]{2,1,0:T(8,128)(2,1)} %param.12) | copy-start | bytes 3145732
  270.6 30.2 %copy-start.10 = (bf16[1,128,4096]{2,1,0:T(8,128)(2,1)S(1)}, bf16[1,128,4096]{2,1,0:T(8,128)(2,1)}, u32[]{:S(2)}) copy-start(bf16[1,128,4096]{2,1,0:T(8,128)(2,1)} %param.10) | copy-start | bytes 3145732
Sparse Core Ops, SparseCore 0:
  269.1 189.1 all-reduce.1
where the time goes:
time: 474 us; the launch traced here: 467 us
  waiting for transfers between devices  226 us (48%)
  matrix products  117 us (25%)
  starting transfers between devices  45.9 us (10%)
  other arithmetic  31.9 us (7%)
  local copies, waits for them, and re-layouts  31.5 us (7%)
  between operations  14.8 us (3%)
    psum x1, waiting for transfers between devices, per_device(): total_taps = lax.psum(tap_part, 'ctx')  155 us
    conv_general_dilated x3, matrix products, depthwise(): lax.conv_general_dilated(extended[None], kernel[:, None, :], (1,), 'VALID...  86.3 us
    dot_general x6, matrix products, contract(): jnp.einsum(form, left, right, precision=lax.Precision.HIGH, preferred_ele...  31 us
    all_to_all x1, waiting for transfers between devices, per_device(): lax.all_to_all(input_part.astype(jnp.bfloat16), 'ctx', split_axis=1, conc...  27.6 us
    ppermute x1, waiting for transfers between devices, passed_along(): return lax.ppermute(value, axis, pairs)  24.9 us
    all_to_all x1, starting transfers between devices, per_device(): lax.all_to_all(long_in.T, 'ctx', split_axis=0, concat_axis=1, tiled=True)  24.9 us
    all_to_all x1, waiting for transfers between devices, per_device(): lax.all_to_all(grad_z.T, 'ctx', split_axis=0, concat_axis=1, tiled=True)  17.8 us
    rev x1, local copies, waits for them, and re-layouts, per_device(): tap_part = depthwise(extended, grad_b)[::-1]  16.6 us
  transfers between devices with their start and end apart: 7, of which 6 were waited for; matrix products, arithmetic and copies ran while one was open for 21% of the time, Pallas kernels for 0%

commit v1 on v0

--- a/solution.py
+++ b/solution.py
@@ -140,7 +140,8 @@
     grad_act = depthwise(jnp.concatenate([grad_b, later], 0), filter_taps)
     input_grad = (grad_u + grad_act * gate_pre).astype(jnp.bfloat16)[None]
     tap_part = depthwise(extended, grad_b)[::-1]
-    total_taps = lax.psum(tap_part, "ctx")
+    pieces = lax.all_gather(tap_part, "ctx", axis=0, tiled=False)
+    total_taps = pieces.sum(axis=0)
     columns = tap_part.shape[1] // lax.axis_size("ctx")
     own_taps = lax.dynamic_slice_in_dim(total_taps, lax.axis_index("ctx") * columns, columns, 1)
     mid_grad = (own_taps * scale).astype(jnp.bfloat16)[None]

time: 474 us -> 760 us (1.60)
  waiting for transfers between devices: 226 us -> 440 us
  other arithmetic: 31.9 us -> 71.2 us
  blocking collectives: 0 us -> 34.4 us
    all_gather x0 -> x1, waiting for transfers between devices: none -> 395 us  [per_device(): pieces = lax.all_gather(tap_part, 'ctx', axis=0, tiled=False)]
    psum x1 -> x0, waiting for transfers between devices: 155 us -> none  [per_device(): total_taps = lax.psum(tap_part, 'ctx')]
    reduce_sum x0 -> x1, other arithmetic: none -> 40.6 us  [per_device(): total_taps = pieces.sum(axis=0)]
    all_to_all x0 -> x1, blocking collectives: none -> 34.4 us  [per_device(): lax.all_to_all(input_part.astype(jnp.bfloat16), 'ctx', split_axis=1, conc...]
    all_to_all x1 -> x0, waiting for transfers between devices: 27.6 us -> none  [per_device(): lax.all_to_all(input_part.astype(jnp.bfloat16), 'ctx', split_axis=1, conc...]
  transfers between devices with their start and end apart: 7 -> 6, of which waited for: 6 -> 6; matrix products, arithmetic and copies ran while one was open for 21% -> 7% of each run, Pallas kernels for 0% -> 0%
where the time goes in v1:
time: 760 us; the launch traced here: 751 us
  waiting for transfers between devices  440 us (58%)
  matrix products  118 us (16%)
  other arithmetic  71.2 us (9%)
  starting transfers between devices  40.3 us (5%)
  blocking collectives  34.4 us (5%)
  local copies, waits for them, and re-layouts  31.6 us (4%)
  between operations  14.8 us (2%)
    all_gather x1, waiting for transfers between devices, per_device(): pieces = lax.all_gather(tap_part, 'ctx', axis=0, tiled=False)  395 us
    conv_general_dilated x3, matrix products, depthwise(): lax.conv_general_dilated(extended[None], kernel[:, None, :], (1,), 'VALID...  87.6 us
    reduce_sum x1, other arithmetic, per_device(): total_taps = pieces.sum(axis=0)  40.6 us
    all_to_all x1, blocking collectives, per_device(): lax.all_to_all(input_part.astype(jnp.bfloat16), 'ctx', split_axis=1, conc...  34.4 us
    dot_general x6, matrix products, contract(): jnp.einsum(form, left, right, precision=lax.Precision.HIGH, preferred_ele...  30.6 us
    ppermute x1, waiting for transfers between devices, passed_along(): return lax.ppermute(value, axis, pairs)  24.9 us
    all_to_all x1, starting transfers between devices, per_device(): lax.all_to_all(long_in.T, 'ctx', split_axis=0, concat_axis=1, tiled=True)  24.9 us
    all_to_all x1, waiting for transfers between devices, per_device(): lax.all_to_all(grad_z.T, 'ctx', split_axis=0, concat_axis=1, tiled=True)  17.5 us
  transfers between devices with their start and end apart: 6, of which 6 were waited for; matrix products, arithmetic and copies ran while one was open for 7% of the time, Pallas kernels for 0%

profile of v1, /device:TPU:8, one launch (start us, length us, event | category | flops | bytes accessed | tf_op | source)
XLA Modules:
  0.0 750.9 jit_solution(6489696355337215958)
XLA Ops:
  7.2 1.9 fusion.24
  9.1 1.2 slice.67
  10.3 2.7 collective-permute-start.1
  13.0 1.2 rev.6
  14.3 0.4 collective-permute-done.1
  14.6 1.5 maximum_bitcast_fusion.13
  16.2 27.4 %convolution_multiply_fusion = f32[1,128,4096]{2,0,1:T(1,128)S(1)} fusion(bf16[1,255,4096]{2,1,0:T(8,128)(2,1)S(1)} %maximum_bitcast_fusion.13, bf16[128,1,4096]{2,0,1:T(8,128)(2,1)S(1)} %bitcast.191), kind=kOutput, calls=%fused_computation.15 | convolution fusion | flops 134742016 | bytes 5234688 | tf_op jit(solution)/shard_map/conv_general_dilated | solution.py:81
  43.7 2.1 fusion.34
  45.8 1.3 copy.55
  47.1 24.9 %all-to-all-start.1 = ((bf16[64,64,128]{2,1,0:T(8,128)(2,1)}), bf16[64,64,128]{2,1,0:T(8,128)(2,1)S(1)}, u32[]{:S(2)}, u32[]{:S(2)}) async-start(bf16[64,64,128]{2,1,0:T(8,128)(2,1)} %bitcast.35), calls=%async_computation.1 | async-start | bytes 2097152 | tf_op jit(solution)/shard_map/all_to_all | solution.py:118
  71.9 0.5 collective-permute-start
  72.5 24.9 %collective-permute-done = bf16[128,4096]{1,0:T(8,128)(2,1)S(1)} collective-permute-done((bf16[128,4096]{1,0:T(8,128)(2,1)}, bf16[128,4096]{1,0:T(8,128)(2,1)S(1)}, u32[]{:S(2)}, u32[]{:S(2)}) %collective-permute-start) | collective-permute-done | bytes 1048608 | tf_op jit(solution)/shard_map/ppermute | solution.py:11
  97.4 1.9 fusion.36
  99.3 1.3 copy.49
  100.8 10.4 %all-to-all-start = ((bf16[64,64,128]{2,1,0:T(8,128)(2,1)}), bf16[64,64,128]{2,1,0:T(8,128)(2,1)}, u32[]{:S(2)}, u32[]{:S(2)}) async-start(bf16[64,64,128]{2,1,0:T(8,128)(2,1)} %bitcast.184), calls=%async_computation | async-start | bytes 2097152 | tf_op jit(solution)/shard_map/all_to_all | solution.py:117
  111.2 0.3 all-gather.3.cloned.1.call-start
  111.6 1.4 negate_bitcast_fusion
  114.7 0.7 maximum_multiply_fusion
  115.4 0.7 fusion.43
  116.1 0.7 copy.130
  116.8 5.7 convolution_bitcast_fusion.1
  122.5 17.5 %all-to-all-done = bf16[64,64,128]{2,1,0:T(8,128)(2,1)} async-done(((bf16[64,64,128]{2,1,0:T(8,128)(2,1)}), bf16[64,64,128]{2,1,0:T(8,128)(2,1)}, u32[]{:S(2)}, u32[]{:S(2)}) %all-to-all-start) | async-done | bytes 1048608 | tf_op jit(solution)/shard_map/all_to_all | solution.py:117
  140.0 3.8 convolution_bitcast_fusion
  143.8 6.4 multiply_subtract_fusion.3
  150.2 6.8 fusion.19
  157.0 4.9 fusion.20
  162.0 2.0 multiply_add_fusion.1
  163.9 5.0 fusion.16
  169.0 1.9 multiply_add_fusion
  170.9 4.4 fusion.33
  175.3 1.1 fusion.92
  176.5 0.7 copy.63
  177.2 34.4 %all_to_all.42 = bf16[64,64,128]{2,0,1:T(8,128)(2,1)S(1)} all-to-all(bf16[64,64,128]{2,0,1:T(8,128)(2,1)S(1)} %copy.63), channel_id=1, replica_groups=mesh['section'=4,'ctx'=64] {'ctx'}, dimensions={1} | all-to-all | bytes 2097152 | tf_op jit(solution)/shard_map/all_to_all | solution.py:134
  211.6 1.6 convert_element_type.251
  213.2 1.9 copy.64
  215.2 2.9 fusion.23
  218.1 30.1 %fusion.13 = f32[1,128,4096]{2,0,1:T(1,128)S(1)} fusion(bf16[1,255,4096]{2,1,0:T(8,128)(2,1)S(1)} %copy-done.15, bf16[128,1,4096]{2,0,1:T(8,128)(2,1)S(1)} %bitcast.185), kind=kOutput, calls=%fused_computation.27 | convolution fusion | flops 134217728 | bytes 5234688 | tf_op jit(solution)/shard_map/conv_general_dilated | solution.py:81
  248.3 3.0 copy.129
  251.3 16.8 %rev.7 = f32[128,4096]{1,0:T(8,128)} reverse(f32[128,4096]{1,0:T(8,128)} %bitcast.183), dimensions={0} | reverse | bytes 4194304 | tf_op jit(solution)/shard_map/rev | solution.py:142
  268.1 1.4 collective-permute-start.2
  269.5 1.3 convert_element_type.242
  270.8 2.1 collective-permute-done.2
  272.9 1.4 maximum_bitcast_fusion.16
  274.4 30.1 %fusion.11 = f32[1,128,4096]{2,0,1:T(1,128)S(1)} fusion(bf16[1,255,4096]{2,1,0:T(8,128)(2,1)S(1)} %maximum_bitcast_fusion.16, bf16[128,1,4096]{2,0,1:T(8,128)(2,1)S(1)} %bitcast.190), kind=kOutput, calls=%fused_computation.25 | convolution fusion | flops 134217728 | bytes 5234688 | tf_op jit(solution)/shard_map/conv_general_dilated | solution.py:81
  304.5 2.8 fusion.35
  307.3 395.1 %all-gather.3.cloned.1.call-done = f32[8192,4096]{1,0:T(8,128)} async-done(((f32[128,4096]{1,0:T(8,128)}), f32[8192,4096]{1,0:T(8,128)}) %all-gather.3.cloned.1.call-update) | async-done | bytes 134217744 | tf_op jit(solution)/shard_map/all_gather | solution.py:143
  702.4 40.6 %reduce_sum.9 = f32[128,4096]{1,0:T(8,128)S(1)} reduce(f32[64,128,4096]{2,1,0:T(8,128)} %bitcast.73, f32[]{:T(128)} %constant.83.clone.1), dimensions={0}, to_apply=%region_0.1 | reduce | flops 33030144 | bytes 136314880 | tf_op jit(solution)/shard_map/reduce_sum | solution.py:144
  743.1 0.7 copy.69
  (60 shorter events, 2.2 us)
Async XLA Ops:
  7.2 5.9 copy-start.16
  10.3 4.3 collective-permute-start.1
  16.2 27.5 %copy-start.14 = (bf16[1,255,4096]{2,1,0:T(8,128)(2,1)}, bf16[1,255,4096]{2,1,0:T(8,128)(2,1)S(1)}, u32[]{:S(2)}) copy-start(bf16[1,255,4096]{2,1,0:T(8,128)(2,1)S(1)} %maximum_bitcast_fusion.13) | copy-start | bytes 6266884
  16.2 27.5 %copy-start.6 = (bf16[1,128,4096]{2,1,0:T(8,128)(2,1)S(1)}, bf16[1,128,4096]{2,1,0:T(8,128)(2,1)}, u32[]{:S(2)}) copy-start(bf16[1,128,4096]{2,1,0:T(8,128)(2,1)} %param.12) | copy-start | bytes 3145732
  16.2 27.5 %copy-start.8 = (bf16[1,128,4096]{2,1,0:T(8,128)(2,1)S(1)}, bf16[1,128,4096]{2,1,0:T(8,128)(2,1)}, u32[]{:S(2)}) copy-start(bf16[1,128,4096]{2,1,0:T(8,128)(2,1)} %param.9) | copy-start | bytes 3145732
  16.2 27.5 %copy-start.10 = (bf16[1,128,4096]{2,1,0:T(8,128)(2,1)S(1)}, bf16[1,128,4096]{2,1,0:T(8,128)(2,1)}, u32[]{:S(2)}) copy-start(bf16[1,128,4096]{2,1,0:T(8,128)(2,1)} %param.11) | copy-start | bytes 3145732
  47.1 53.8 %all-to-all-start.1 = ((bf16[64,64,128]{2,1,0:T(8,128)(2,1)}), bf16[64,64,128]{2,1,0:T(8,128)(2,1)S(1)}, u32[]{:S(2)}, u32[]{:S(2)}) async-start(bf16[64,64,128]{2,1,0:T(8,128)(2,1)} %bitcast.35), calls=%async_computation.1 | async-start | bytes 2097152 | tf_op jit(solution)/shard_map/all_to_all | solution.py:118
  71.9 25.4 %collective-permute-start = (bf16[128,4096]{1,0:T(8,128)(2,1)}, bf16[128,4096]{1,0:T(8,128)(2,1)S(1)}, u32[]{:S(2)}, u32[]{:S(2)}) collective-permute-start(bf16[128,4096]{1,0:T(8,128)(2,1)} %bitcast.192), channel_id=1, source_target_pairs={{0,192},{64,0},{128,64},{192,128},{1,193},{65,1},{129,65},{193,129... | collective-permute-start | bytes 3145736 | tf_op jit(solution)/shard_map/ppermute | solution.py:11
  97.4 117.8 %copy-start.4 = (bf16[128,4096]{1,0:T(8,128)(2,1)}, bf16[128,4096]{1,0:T(8,128)(2,1)S(1)}, u32[]{:S(2)}) copy-start(bf16[128,4096]{1,0:T(8,128)(2,1)S(1)} %collective-permute-done) | copy-start | bytes 3145732
  100.8 39.1 %all-to-all-start = ((bf16[64,64,128]{2,1,0:T(8,128)(2,1)}), bf16[64,64,128]{2,1,0:T(8,128)(2,1)}, u32[]{:S(2)}, u32[]{:S(2)}) async-start(bf16[64,64,128]{2,1,0:T(8,128)(2,1)} %bitcast.184), calls=%async_computation | async-start | bytes 2097152 | tf_op jit(solution)/shard_map/all_to_all | solution.py:117
  111.2 591.2 %all-gather.3.cloned.1.call-start = ((), (), s32[]{:S(2)}) async-start(), calls=%async_computation.3 | async-start | bytes 136314880 | tf_op jit(solution)/shard_map/all_gather | solution.py:143
  114.7 2.1 copy-start.18
  114.7 2.1 copy-start.19
  140.0 3.8 copy-start
  150.2 6.8 copy-start.3
  161.9 2.0 copy-start.22
  161.9 2.0 copy-start.23
  168.9 1.9 copy-start.20
  168.9 1.9 copy-start.21
  215.1 33.1 %copy-start.1 = (f32[4096,128]{0,1:T(8,128)}, f32[4096,128]{0,1:T(8,128)S(1)}, u32[]{:S(2)}) copy-start(f32[4096,128]{0,1:T(8,128)S(1)} %copy.64) | copy-start | bytes 6291460
  215.2 3.0 copy-start.15
  218.1 30.2 %copy-start.12 = (bf16[128,4096]{1,0:T(8,128)(2,1)}, bf16[128,4096]{1,0:T(8,128)(2,1)S(1)}, u32[]{:S(2)}) copy-start(bf16[128,4096]{1,0:T(8,128)(2,1)S(1)} %fusion.23) | copy-start | bytes 3145732
  251.3 16.8 %copy-start.13 = (bf16[128,4096]{1,0:T(8,128)(2,1)S(1)}, bf16[128,4096]{1,0:T(8,128)(2,1)}, u32[]{:S(2)}) copy-start(bf16[128,4096]{1,0:T(8,128)(2,1)} %copy-done.12) | copy-start | bytes 3145732
  251.3 18.2 %copy-start.9 = (bf16[64,1,64,128]{3,2,1,0:T(8,128)(2,1)S(1)}, bf16[64,1,64,128]{3,2,1,0:T(8,128)(2,1)}, u32[]{:S(2)}) copy-start(bf16[64,1,64,128]{3,2,1,0:T(8,128)(2,1)} %get-tuple-element.14) | copy-start | bytes 3145732
  268.0 6.3 copy-start.17
  268.1 4.8 collective-permute-start.2
  274.3 30.2 %copy-start.2 = (f32[4096,128]{0,1:T(8,128)S(1)}, f32[4096,128]{0,1:T(8,128)}, u32[]{:S(2)}) copy-start(f32[4096,128]{0,1:T(8,128)} %copy-done.1) | copy-start | bytes 6291460
  274.3 30.2 %copy-start.5 = (bf16[128,4096]{1,0:T(8,128)(2,1)S(1)}, bf16[128,4096]{1,0:T(8,128)(2,1)}, u32[]{:S(2)}) copy-start(bf16[128,4096]{1,0:T(8,128)(2,1)} %copy-done.4) | copy-start | bytes 3145732
  274.3 30.2 %copy-start.7 = (bf16[1,128,4096]{2,1,0:T(8,128)(2,1)S(1)}, bf16[1,128,4096]{2,1,0:T(8,128)(2,1)}, u32[]{:S(2)}) copy-start(bf16[1,128,4096]{2,1,0:T(8,128)(2,1)} %param.12) | copy-start | bytes 3145732
  274.3 30.2 %copy-start.11 = (bf16[1,128,4096]{2,1,0:T(8,128)(2,1)S(1)}, bf16[1,128,4096]{2,1,0:T(8,128)(2,1)}, u32[]{:S(2)}) copy-start(bf16[1,128,4096]{2,1,0:T(8,128)(2,1)} %param.10) | copy-start | bytes 3145732
Sparse Core Ops, SparseCore 0:
  268.2 434.1 all-gather.2
